TPU v7x, 256 devices: a whole 4x4x8 slice. The times are simulated.
256 devices in a mesh: section: 8 (over z_lo, core), vocab: 32 (over y, z_hi, x).
Axes of the slice: x: 4, y: 4, z: 8 (z_hi: 2, z_lo: 4; z = z_hi * 4 + z_lo), core: 2. Of those that a mesh axis runs over, the one named last changes fastest.
Arguments:
- hidden: bfloat16 [8, 512, 8192], P('section', None, 'vocab'), may hold values from -160 to 160
- final_hidden: bfloat16 [512, 8192], P('section', 'vocab'), may hold values from -160 to 160
- row_pick: int32 [8, 128], P('section'), may hold values from 0 to 511
- trans_weight: bfloat16 [8, 8192, 8192], P('section', None, 'vocab'), may hold values from -0.0625 to 0.0625
- trans_bias: bfloat16 [8, 8192], P('section', 'vocab'), may hold values from -6 to 6
- norm_gain: bfloat16 [8192], P('vocab'), may hold values from 0.5 to 1.5
- unembed: bfloat16 [8192, 16384], P('section', 'vocab'), may hold values from -100 to 100
Outputs:
- grad_weight: bfloat16 [8, 8192, 8192], P('section', None, 'vocab')
- grad_bias: float32 [8, 8192], P('section', 'vocab')
- kl_mean: float32 [8], P('section')
All inputs are finite; a program needn't handle non-finite values.
Results may differ from a plain program's by a relative error of at most 0.024.
Values may be sent and summed in bfloat16 or wider, within the bound.
A program may use at most 64 MiB of HBM per device.

v0:
```python
import jax
import jax.numpy as jnp
from jax import lax
from jax.sharding import PartitionSpec as P

epsilon = 1e-05


def combined_all(value, axis, join):
    pieces = jax.tree.map(lambda part: lax.all_gather(part, axis), value)
    head = jax.tree.map(lambda part: part[0], pieces)
    tail = jax.tree.map(lambda part: part[1:], pieces)
    so_far, _ = lax.scan(lambda so_far, section: (join(so_far, section), None), head, tail)
    return so_far


def combine_totals(first, second):
    trans_max = jnp.maximum(first[0], second[0])
    trans_sum = first[1] * jnp.exp(first[0] - trans_max) + second[1] * jnp.exp(
        second[0] - trans_max
    )
    target_max = jnp.maximum(first[2], second[2])
    target_sum = first[3] * jnp.exp(first[2] - target_max) + second[3] * jnp.exp(
        second[2] - target_max
    )
    return (trans_max, trans_sum, target_max, target_sum)


def local_totals(logits):
    highest = jnp.max(logits, axis=-1)
    return (highest, jnp.sum(jnp.exp(logits - highest[:, None]), axis=-1))


def per_device(hidden, final_hidden, row_pick, trans_weight, trans_bias, norm_gain, unembed):
    gain_cols = norm_gain.astype(jnp.float32)
    width = trans_weight.shape[1]
    row_count = row_pick.shape[1]
    unembed_full = lax.all_gather(unembed, "section", axis=0, tiled=True)
    final_cols = lax.all_gather(final_hidden, "section", axis=0, tiled=True)
    picked = row_pick[0]
    input_cols = hidden[0][picked]
    inputs = lax.all_gather(input_cols, "vocab", axis=1, tiled=True)
    trans = (
        input_cols.astype(jnp.float32)
        + jnp.dot(inputs, trans_weight[0], preferred_element_type=jnp.float32)
        + trans_bias[0].astype(jnp.float32)
    )
    finals = final_cols[picked].astype(jnp.float32)
    trans_total, final_total = lax.psum(
        (jnp.sum(trans * trans, axis=-1), jnp.sum(finals * finals, axis=-1)), "vocab"
    )
    trans_scale = lax.rsqrt(trans_total / width + epsilon)
    final_scale = lax.rsqrt(final_total / width + epsilon)
    normed = (trans * trans_scale[:, None] * gain_cols).astype(jnp.bfloat16)
    target = (finals * final_scale[:, None] * gain_cols).astype(jnp.bfloat16)
    slab_rows = unembed_full
    logits = jnp.dot(
        lax.all_gather(normed, "vocab", axis=1, tiled=True),
        slab_rows,
        preferred_element_type=jnp.float32,
    )
    target_logits = jnp.dot(
        lax.all_gather(target, "vocab", axis=1, tiled=True),
        slab_rows,
        preferred_element_type=jnp.float32,
    )
    trans_max, trans_sum = local_totals(logits)
    target_max, target_sum = local_totals(target_logits)
    totals = combined_all((trans_max, trans_sum, target_max, target_sum), "vocab", combine_totals)
    log_trans = logits - (totals[0] + jnp.log(totals[1]))[:, None]
    log_target = target_logits - (totals[2] + jnp.log(totals[3]))[:, None]
    probs = jnp.exp(log_target)
    kl_part = jnp.sum(probs * (log_target - log_trans), axis=-1)
    dlogits = (jnp.exp(log_trans) - probs).astype(jnp.bfloat16)
    kl_rows = lax.psum(kl_part, "vocab")
    slab_rows = unembed_full
    dnormed_cols = lax.psum_scatter(
        lax.dot_general(
            slab_rows, dlogits, (((1,), (1,)), ((), ())), preferred_element_type=jnp.float32
        ).astype(jnp.bfloat16),
        "vocab",
        scatter_dimension=0,
        tiled=True,
    ).astype(jnp.float32)
    trans_cols = trans.T
    scaled_cols = dnormed_cols * gain_cols[:, None]
    product = lax.psum(jnp.sum(scaled_cols * trans_cols, axis=0), "vocab") / width
    dtrans_cols = trans_scale[None, :] * (
        scaled_cols - trans_cols * (trans_scale * trans_scale * product)[None, :]
    )
    grad_weights = [
        lax.dot_general(
            inputs,
            dtrans_cols.astype(jnp.bfloat16),
            (((0,), (1,)), ((), ())),
            preferred_element_type=jnp.float32,
        ).astype(jnp.bfloat16)
    ]
    grad_biases = [jnp.sum(dtrans_cols, axis=1)]
    kl_values = [jnp.sum(kl_rows) / row_count]
    return (jnp.stack(grad_weights), jnp.stack(grad_biases), jnp.stack(kl_values))


def solution(mesh):
    placed = (
        P("section", None, "vocab"),
        P("section", "vocab"),
        P("section", None),
        P("section", None, "vocab"),
        P("section", "vocab"),
        P("vocab"),
        P("section", "vocab"),
    )
    return jax.shard_map(
        per_device,
        mesh=mesh,
        in_specs=placed,
        out_specs=(P("section", None, "vocab"), P("section", "vocab"), P("section")),
        check_vma=False,
    )
```

profile of v0, /device:TPU:2, one launch (start us, length us, event | category | flops | bytes accessed | tf_op | source)
XLA Modules:
  0.0 1215.9 jit_solution(14653384392186049527)
XLA Ops:
  7.2 0.0 copy-start
  7.2 0.0 all-gather.20.cloned.1.call-start
  7.2 0.7 fusion.34
  7.9 0.2 copy-done
  8.1 1.5 gather_fusion
  9.6 0.0 all-gather.20.cloned.1.call-update
  9.6 0.0 all-gather.14.cloned.1.call-start
  9.7 0.7 add.75
  10.4 0.7 convert_element_type.38
  11.0 15.4 %all_gather.46 = bf16[512,256]{1,0:T(8,128)(2,1)S(1)} all-gather(bf16[64,256]{1,0:T(8,128)(2,1)} %param.10), channel_id=1, replica_groups=mesh['section'=8,'vocab'=32] {'section'}, dimensions={0}, use_global_device_ids=true | all-gather | bytes 294912 | tf_op jit(solution)/shard_map/all_gather | solution.py:39
  26.4 0.8 gather_fusion.1
  27.2 0.1 fusion.20
  27.3 84.5 %all-gather.20.cloned.1.call-done = bf16[128,8192]{1,0:T(8,128)(2,1)} async-done(((bf16[128,256]{1,0:T(8,128)(2,1)}), bf16[128,8192]{1,0:T(8,128)(2,1)}) %all-gather.20.cloned.1.call-update) | async-done | bytes 2097168 | tf_op jit(solution)/shard_map/all_gather | solution.py:42
  111.8 3.7 multiply_reduce_fusion.1
  115.4 109.8 %all-reduce.1 = (f32[128]{0:T(128)S(1)}, f32[128]{0:T(128)S(1)}) all-reduce(f32[128]{0:T(128)S(1)} %fusion.20, f32[128]{0:T(128)S(1)} %get-tuple-element.87), channel_id=1, replica_groups=mesh['section'=8,'vocab'=32] {'vocab'}, use_global_device_ids=true, to_apply=%region_5.0 | all-reduce | flops 256 | bytes 2048 | tf_op jit(solution)/shard_map/psum | solution.py:49
  225.3 0.8 multiply_convert_fusion
  226.1 0.0 all-gather.14.cloned.1.call-update
  226.1 0.0 all-gather.16.cloned.1.call-start
  226.1 0.7 all-gather.16.cloned.1.call-update
  226.8 0.0 all-gather.18.cloned.1.call-start
  226.9 0.5 all-gather.18.cloned.1.call-update
  227.4 0.0 reduce-scatter.2.cloned.1.call-start
  227.4 90.7 %all-gather.14.cloned.1.call-done = bf16[128,8192]{1,0:T(8,128)(2,1)} async-done(((bf16[128,256]{1,0:T(8,128)(2,1)}), bf16[128,8192]{1,0:T(8,128)(2,1)}) %all-gather.14.cloned.1.call-update) | async-done | bytes 2097168 | tf_op jit(solution)/shard_map/all_gather | solution.py:58
  318.2 91.2 %all-gather.16.cloned.1.call-done = bf16[8192,512]{1,0:T(8,128)(2,1)} async-done(((bf16[1024,512]{1,0:T(8,128)(2,1)}), bf16[8192,512]{1,0:T(8,128)(2,1)}) %all-gather.16.cloned.1.call-update) | async-done | bytes 8388624 | tf_op jit(solution)/shard_map/all_gather | solution.py:38
  409.4 5.4 fusion.37
  414.8 107.7 %all-gather.5 = f32[32,1,128]{2,1,0:T(1,128)S(1)} all-gather(f32[1,1,128]{2,1,0:T(1,128)S(1)} %bitcast.100), channel_id=3, replica_groups=mesh['section'=8,'vocab'=32] {'vocab'}, dimensions={0}, use_global_device_ids=true | all-gather | bytes 16896 | tf_op jit(solution)/shard_map/all_gather | solution.py:10
  522.5 0.2 exponential_reduce_fusion.1
  522.6 115.5 %all-gather.6 = f32[32,1,128]{2,1,0:T(1,128)S(1)} all-gather(f32[1,1,128]{2,1,0:T(1,128)S(1)} %bitcast.102), channel_id=4, replica_groups=mesh['section'=8,'vocab'=32] {'vocab'}, dimensions={0}, use_global_device_ids=true | all-gather | bytes 16896 | tf_op jit(solution)/shard_map/all_gather | solution.py:10
  638.2 0.0 all-gather.18.cloned.1.call-done
  638.2 5.4 fusion.38
  643.6 106.6 %all-gather.7 = f32[32,1,128]{2,1,0:T(1,128)S(1)} all-gather(f32[1,1,128]{2,1,0:T(1,128)S(1)} %bitcast.99), channel_id=5, replica_groups=mesh['section'=8,'vocab'=32] {'vocab'}, dimensions={0}, use_global_device_ids=true | all-gather | bytes 16896 | tf_op jit(solution)/shard_map/all_gather | solution.py:10
  750.1 0.2 exponential_reduce_fusion
  750.3 108.6 %all-gather.8 = f32[32,1,128]{2,1,0:T(1,128)S(1)} all-gather(f32[1,1,128]{2,1,0:T(1,128)S(1)} %bitcast.103), channel_id=6, replica_groups=mesh['section'=8,'vocab'=32] {'vocab'}, dimensions={0}, use_global_device_ids=true | all-gather | bytes 16896 | tf_op jit(solution)/shard_map/all_gather | solution.py:10
  858.9 1.5 while.16
  860.5 7.5 fusion.11
  868.0 0.0 copy-start.1
  868.0 0.0 reduce-scatter.2.cloned.1.call-update
  868.0 0.2 multiply_reduce_fusion
  868.3 214.5 %reduce-scatter.2.cloned.1.call-done = bf16[256,128]{0,1:T(8,128)(2,1)} async-done(((bf16[8192,128]{0,1:T(8,128)(2,1)}), bf16[256,128]{0,1:T(8,128)(2,1)}) %reduce-scatter.2.cloned.1.call-update) | async-done | bytes 65552 | tf_op jit(solution)/shard_map/reduce_scatter | solution.py:77
  1082.8 0.0 copy-start.2
  1082.8 1.0 fusion.23
  1083.8 118.2 %all-reduce = (f32[128]{0:T(128)S(1)}, f32[128]{0:T(128)S(1)}) all-reduce(f32[128]{0:T(128)S(1)} %fusion.23, f32[128]{0:T(128)S(1)} %multiply_reduce_fusion), channel_id=1, replica_groups=mesh['section'=8,'vocab'=32] {'vocab'}, use_global_device_ids=true, to_apply=%region_12.13 | all-reduce | flops 256 | bytes 2048 | tf_op jit(solution)/shard_map/psum | solution.py:87
  1202.1 0.6 reduce_sum.79
  1203.3 0.0 copy-done.1
  1203.4 4.2 fusion.10
  1207.5 0.0 copy-done.2
  1207.5 0.7 fusion.28
  (48 shorter events, 1.1 us)
Async XLA Ops:
  7.2 1.0 copy-start
  7.2 104.6 %all-gather.20.cloned.1.call-start = ((), (), s32[]{:S(2)}) async-start(), calls=%async_computation.5 | async-start | bytes 2162688 | tf_op jit(solution)/shard_map/all_gather | solution.py:42
  9.6 308.6 %all-gather.14.cloned.1.call-start = ((), (), s32[]{:S(2)}) async-start(), calls=%async_computation.1 | async-start | bytes 2162688 | tf_op jit(solution)/shard_map/all_gather | solution.py:58
  226.1 183.3 %all-gather.16.cloned.1.call-start = ((), (), s32[]{:S(2)}) async-start(), calls=%async_computation.2 | async-start | bytes 9437184 | tf_op jit(solution)/shard_map/all_gather | solution.py:38
  226.8 411.4 %all-gather.18.cloned.1.call-start = ((), (), s32[]{:S(2)}) async-start(), calls=%async_computation.3 | async-start | bytes 2162688 | tf_op jit(solution)/shard_map/all_gather | solution.py:63
  227.4 855.4 %reduce-scatter.2.cloned.1.call-start = ((), (), s32[]{:S(2)}) async-start(), calls=%async_computation.4 | async-start | bytes 2162688 | tf_op jit(solution)/shard_map/reduce_scatter | solution.py:77
  868.0 335.3 %copy-start.1 = (bf16[128,8192]{1,0:T(8,128)(2,1)S(1)}, bf16[128,8192]{1,0:T(8,128)(2,1)}, u32[]{:S(2)}) copy-start(bf16[128,8192]{1,0:T(8,128)(2,1)} %all-gather.20.cloned.1.call-done) | copy-start | bytes 6291460
  1082.8 124.7 %copy-start.2 = (bf16[256,128]{0,1:T(8,128)(2,1)S(1)}, bf16[256,128]{0,1:T(8,128)(2,1)}, u32[]{:S(2)}) copy-start(bf16[256,128]{0,1:T(8,128)(2,1)} %reduce-scatter.2.cloned.1.call-done) | copy-start | bytes 196612
Sparse Core Ops, SparseCore 0:
  11.8 99.9 all-gather.19
  226.2 91.9 all-gather.13
  320.0 89.4 all-gather.15
  412.5 95.5 all-gather.17
  868.2 214.5 reduce-scatter.1
where the time goes:
time: 1220 us
  blocking collectives  682 us (56%)
  waiting for transfers between devices  482 us (40%)
  matrix products  26.1 us (2%)
  between operations  15.7 us (1%)
    all_gather x4, blocking collectives, combined_all(): pieces = jax.tree.map(lambda part: lax.all_gather(part, axis), value)  438 us
    reduce_scatter x1, waiting for transfers between devices, per_device(): lax.psum_scatter(lax.dot_general(slab_rows, dlogits, (((1,), (1,)), ((),...  215 us
    psum x1, blocking collectives, per_device(): lax.psum(jnp.sum(scaled_cols * trans_cols, axis=0), 'vocab') / width  118 us
    psum x1, blocking collectives, per_device(): lax.psum((jnp.sum(trans * trans, axis=-1), jnp.sum(finals * finals, axis=...  110 us
    all_gather x1, waiting for transfers between devices, per_device(): unembed_full = lax.all_gather(unembed, 'section', axis=0, tiled=True)  91.2 us
    all_gather x1, waiting for transfers between devices, per_device(): lax.all_gather(normed, 'vocab', axis=1, tiled=True)  90.7 us
    all_gather x1, waiting for transfers between devices, per_device(): inputs = lax.all_gather(input_cols, 'vocab', axis=1, tiled=True)  84.5 us
  transfers between devices with their start and end apart: 5, of which 4 were waited for; matrix products, arithmetic and copies ran while one was open for 1% of the time, Pallas kernels for 0%

commit v1 on v0

--- a/solution.py
+++ b/solution.py
@@ -55,7 +55,9 @@
     target = (finals * final_scale[:, None] * gain_cols).astype(jnp.bfloat16)
     slab_rows = unembed_full
     logits = jnp.dot(
-        lax.all_gather(normed, "vocab", axis=1, tiled=True),
+        jnp.concatenate(
+            lax.all_to_all(jnp.stack([normed] * lax.axis_size("vocab")), "vocab", 0, 0), axis=1
+        ),
         slab_rows,
         preferred_element_type=jnp.float32,
     )

time: 1220 us -> 1080 us (0.89)
  waiting for transfers between devices: 482 us -> 340 us
    all_gather x1, waiting for transfers between devices: 91.2 us -> 0.01 us  [per_device(): unembed_full = lax.all_gather(unembed, 'section', axis=0, tiled=True)]
    all_gather x1 -> x0, waiting for transfers between devices: 90.7 us -> none  [per_device(): lax.all_gather(normed, 'vocab', axis=1, tiled=True)]
    all_to_all x0 -> x1, waiting for transfers between devices: none -> 36.8 us  [per_device(): lax.all_to_all(jnp.stack([normed] * lax.axis_size('vocab')), 'vocab', 0, 0)]
  transfers between devices with their start and end apart: 5 -> 5, of which waited for: 4 -> 3; matrix products, arithmetic and copies ran while one was open for 1% -> 1% of each run, Pallas kernels for 0% -> 0%
where the time goes in v1:
time: 1080 us
  blocking collectives  685 us (63%)
  waiting for transfers between devices  340 us (31%)
  matrix products  25.5 us (2%)
  between operations  15.6 us (1%)
    all_gather x4, blocking collectives, combined_all(): pieces = jax.tree.map(lambda part: lax.all_gather(part, axis), value)  438 us
    reduce_scatter x1, waiting for transfers between devices, per_device(): lax.psum_scatter(lax.dot_general(slab_rows, dlogits, (((1,), (1,)), ((),...  218 us
    psum x1, blocking collectives, per_device(): lax.psum(jnp.sum(scaled_cols * trans_cols, axis=0), 'vocab') / width  118 us
    psum x1, blocking collectives, per_device(): lax.psum((jnp.sum(trans * trans, axis=-1), jnp.sum(finals * finals, axis=...  112 us
    all_gather x1, waiting for transfers between devices, per_device(): inputs = lax.all_gather(input_cols, 'vocab', axis=1, tiled=True)  83.7 us
    all_to_all x1, waiting for transfers between devices, per_device(): lax.all_to_all(jnp.stack([normed] * lax.axis_size('vocab')), 'vocab', 0, 0)  36.8 us
  transfers between devices with their start and end apart: 5, of which 3 were waited for; matrix products, arithmetic and copies ran while one was open for 1% of the time, Pallas kernels for 0%

profile of v1, /device:TPU:2, one launch (start us, length us, event | category | flops | bytes accessed | tf_op | source)
XLA Modules:
  0.0 1081.8 jit_solution(18250232074506729812)
XLA Ops:
  7.2 0.0 copy-start
  7.2 0.0 all-gather.17.cloned.1.call-start
  7.2 0.7 fusion.34
  7.9 0.2 copy-done
  8.1 1.5 gather_fusion
  9.6 0.0 all-gather.17.cloned.1.call-update
  9.6 0.0 all-gather.13.cloned.1.call-start
  9.7 0.7 all-gather.13.cloned.1.call-update
  10.4 0.7 add.75
  11.1 15.4 %all_gather.42 = bf16[512,256]{1,0:T(8,128)(2,1)S(1)} all-gather(bf16[64,256]{1,0:T(8,128)(2,1)} %param.10), channel_id=1, replica_groups=mesh['section'=8,'vocab'=32] {'section'}, dimensions={0}, use_global_device_ids=true | all-gather | bytes 294912 | tf_op jit(solution)/shard_map/all_gather | solution.py:39
  26.4 0.8 gather_fusion.1
  27.3 0.7 convert_element_type.38
  27.9 0.1 fusion.20
  28.0 83.7 %all-gather.17.cloned.1.call-done = bf16[128,8192]{1,0:T(8,128)(2,1)} async-done(((bf16[128,256]{1,0:T(8,128)(2,1)}), bf16[128,8192]{1,0:T(8,128)(2,1)}) %all-gather.17.cloned.1.call-update) | async-done | bytes 2097168 | tf_op jit(solution)/shard_map/all_gather | solution.py:42
  111.8 3.7 multiply_reduce_fusion.1
  115.4 112.4 %all-reduce.1 = (f32[128]{0:T(128)S(1)}, f32[128]{0:T(128)S(1)}) all-reduce(f32[128]{0:T(128)S(1)} %fusion.20, f32[128]{0:T(128)S(1)} %get-tuple-element.87), channel_id=1, replica_groups=mesh['section'=8,'vocab'=32] {'vocab'}, use_global_device_ids=true, to_apply=%region_5.0 | all-reduce | flops 256 | bytes 2048 | tf_op jit(solution)/shard_map/psum | solution.py:49
  227.9 0.7 multiply_convert_fusion
  228.6 0.1 copy.11
  228.7 1.8 stack.8
  230.5 3.8 all-to-all-start
  234.3 0.0 all-gather.15.cloned.1.call-start
  234.4 0.7 all-gather.15.cloned.1.call-update
  235.1 0.0 reduce-scatter.2.cloned.1.call-start
  235.1 36.8 %all-to-all-done = bf16[32,128,256]{1,2,0:T(8,128)(2,1)S(1)} async-done(((bf16[32,128,256]{1,2,0:T(8,128)(2,1)}), bf16[32,128,256]{1,2,0:T(8,128)(2,1)S(1)}, u32[]{:S(2)}, u32[]{:S(2)}) %all-to-all-start) | async-done | bytes 2097184 | tf_op jit(solution)/shard_map/all_to_all | solution.py:59
  272.0 0.0 all-gather.13.cloned.1.call-done
  272.0 4.8 fusion.37
  276.7 0.2 exponential_reduce_fusion.1
  276.9 108.7 %all-gather.6 = f32[32,1,128]{2,1,0:T(1,128)S(1)} all-gather(f32[1,1,128]{2,1,0:T(1,128)S(1)} %bitcast.106), channel_id=4, replica_groups=mesh['section'=8,'vocab'=32] {'vocab'}, dimensions={0}, use_global_device_ids=true | all-gather | bytes 16896 | tf_op jit(solution)/shard_map/all_gather | solution.py:10
  385.6 0.0 all-gather.15.cloned.1.call-done
  385.6 5.4 fusion.38
  391.0 0.2 exponential_reduce_fusion
  391.2 114.5 %all-gather.8 = f32[32,1,128]{2,1,0:T(1,128)S(1)} all-gather(f32[1,1,128]{2,1,0:T(1,128)S(1)} %bitcast.107), channel_id=6, replica_groups=mesh['section'=8,'vocab'=32] {'vocab'}, dimensions={0}, use_global_device_ids=true | all-gather | bytes 16896 | tf_op jit(solution)/shard_map/all_gather | solution.py:10
  505.7 106.6 %all-gather.5 = f32[32,1,128]{2,1,0:T(1,128)S(1)} all-gather(f32[1,1,128]{2,1,0:T(1,128)S(1)} %bitcast.103), channel_id=3, replica_groups=mesh['section'=8,'vocab'=32] {'vocab'}, dimensions={0}, use_global_device_ids=true | all-gather | bytes 16896 | tf_op jit(solution)/shard_map/all_gather | solution.py:10
  612.3 108.6 %all-gather.7 = f32[32,1,128]{2,1,0:T(1,128)S(1)} all-gather(f32[1,1,128]{2,1,0:T(1,128)S(1)} %bitcast.104), channel_id=5, replica_groups=mesh['section'=8,'vocab'=32] {'vocab'}, dimensions={0}, use_global_device_ids=true | all-gather | bytes 16896 | tf_op jit(solution)/shard_map/all_gather | solution.py:10
  720.9 1.5 while.16
  722.4 7.5 fusion.11
  730.0 0.0 copy-start.1
  730.0 0.0 reduce-scatter.2.cloned.1.call-update
  730.0 0.2 multiply_reduce_fusion
  730.2 217.6 %reduce-scatter.2.cloned.1.call-done = bf16[256,128]{0,1:T(8,128)(2,1)} async-done(((bf16[8192,128]{0,1:T(8,128)(2,1)}), bf16[256,128]{0,1:T(8,128)(2,1)}) %reduce-scatter.2.cloned.1.call-update) | async-done | bytes 65552 | tf_op jit(solution)/shard_map/reduce_scatter | solution.py:79
  947.8 0.9 fusion.23
  948.8 118.4 %all-reduce = (f32[128]{0:T(128)S(1)}, f32[128]{0:T(128)S(1)}) all-reduce(f32[128]{0:T(128)S(1)} %fusion.23, f32[128]{0:T(128)S(1)} %multiply_reduce_fusion), channel_id=1, replica_groups=mesh['section'=8,'vocab'=32] {'vocab'}, use_global_device_ids=true, to_apply=%region_12.13 | all-reduce | flops 256 | bytes 2048 | tf_op jit(solution)/shard_map/psum | solution.py:89
  1067.2 0.6 reduce_sum.79
  1068.4 1.5 fusion.28
  1069.9 0.0 copy-done.1
  1069.9 4.2 fusion.10
  (48 shorter events, 1.1 us)
Async XLA Ops:
  7.2 1.0 copy-start
  7.2 104.6 %all-gather.17.cloned.1.call-start = ((), (), s32[]{:S(2)}) async-start(), calls=%async_computation.5 | async-start | bytes 2162688 | tf_op jit(solution)/shard_map/all_gather | solution.py:42
  9.6 262.3 %all-gather.13.cloned.1.call-start = ((), (), s32[]{:S(2)}) async-start(), calls=%async_computation.2 | async-start | bytes 9437184 | tf_op jit(solution)/shard_map/all_gather | solution.py:38
  230.5 41.4 %all-to-all-start = ((bf16[32,128,256]{1,2,0:T(8,128)(2,1)}), bf16[32,128,256]{1,2,0:T(8,128)(2,1)S(1)}, u32[]{:S(2)}, u32[]{:S(2)}) async-start(bf16[32,128,256]{1,2,0:T(8,128)(2,1)} %stack.8), calls=%async_computation | async-start | bytes 4194304 | tf_op jit(solution)/shard_map/all_to_all | solution.py:59
  234.3 151.3 %all-gather.15.cloned.1.call-start = ((), (), s32[]{:S(2)}) async-start(), calls=%async_computation.3 | async-start | bytes 2162688 | tf_op jit(solution)/shard_map/all_gather | solution.py:65
  235.1 712.7 %reduce-scatter.2.cloned.1.call-start = ((), (), s32[]{:S(2)}) async-start(), calls=%async_computation.4 | async-start | bytes 2162688 | tf_op jit(solution)/shard_map/reduce_scatter | solution.py:79
  730.0 340.0 %copy-start.1 = (bf16[128,8192]{1,0:T(8,128)(2,1)S(1)}, bf16[128,8192]{1,0:T(8,128)(2,1)}, u32[]{:S(2)}) copy-start(bf16[128,8192]{1,0:T(8,128)(2,1)} %all-gather.17.cloned.1.call-done) | copy-start | bytes 6291460
Sparse Core Ops, SparseCore 0:
  11.8 99.9 all-gather.16
  113.6 89.4 all-gather.12
  238.4 107.1 all-gather.14
  730.1 217.6 reduce-scatter.1
